TPU v7x, 512 devices: a whole 4x4x16 slice. The times are simulated.
512 devices in a mesh: grid: 32 (over x, y, core), band: 16 (over z).
Axes of the slice: x: 4, y: 4, z: 16, core: 2. Of those that a mesh axis runs over, the one named last changes fastest.
Arguments:
- orbitals: bfloat16 [32768, 512], P('grid', 'band'), may hold values from -6 to 6
- rotation: bfloat16 [512, 32768], P('grid', 'band'), may hold values from -0.25 to 0.25
Outputs:
- rotated: bfloat16 [32768, 32768], P('grid', 'band')
All inputs are finite; a program needn't handle non-finite values.
Results may differ from a plain program's by a relative error of at most 0.001.
Values may be sent and summed in bfloat16 or wider, within the bound.
No kernel may reach another device: no remote copies, remote signals or barrier semaphores. Data moves between devices by JAX's collectives and lax.ppermute only.
A program may use at most 64 MiB of HBM per device.

v0:
```python
import jax
import jax.numpy as jnp
from jax import lax
from jax.sharding import PartitionSpec as P


def on_device(orbitals, rotation):
    all_cols = lax.all_gather(orbitals, "band", axis=1, tiled=True)
    all_rows = lax.all_gather(rotation, "grid", axis=0, tiled=True)
    total = jnp.dot(all_cols, all_rows, preferred_element_type=jnp.float32)
    return total.astype(jnp.bfloat16)


def solution(mesh):
    in_specs = (P("grid", "band"), P("grid", "band"))
    out_specs = P("grid", "band")
    return jax.shard_map(
        on_device, mesh=mesh, in_specs=in_specs, out_specs=out_specs, check_vma=False
    )
```

profile of v0, /device:TPU:1, one launch (start us, length us, event | category | flops | bytes accessed | tf_op | source)
XLA Modules:
  0.0 158.6 jit_solution(7569212816232975436)
XLA Ops:
  6.5 0.0 all-gather.3.cloned.1.call-start
  6.5 0.7 all-gather.3.cloned.1.call-update
  7.3 0.0 all-gather.5.cloned.1.call-start
  7.3 0.7 all-gather.5.cloned.1.call-update
  8.0 68.3 %all-gather.3.cloned.1.call-done = bf16[1024,512]{0,1:T(8,128)(2,1)} async-done(((bf16[1024,32]{0,1:T(8,128)(2,1)}), bf16[1024,512]{0,1:T(8,128)(2,1)}) %all-gather.3.cloned.1.call-update) | async-done | bytes 1048592 | tf_op jit(solution)/shard_map/all_gather | solution.py:8
  76.3 69.1 %all-gather.5.cloned.1.call-done = bf16[512,2048]{1,0:T(8,128)(2,1)} async-done(((bf16[16,2048]{1,0:T(8,128)(2,1)}), bf16[512,2048]{1,0:T(8,128)(2,1)}) %all-gather.5.cloned.1.call-update) | async-done | bytes 2097168 | tf_op jit(solution)/shard_map/all_gather | solution.py:9
  145.4 6.3 %convolution_convert_fusion = bf16[1024,2048]{1,0:T(8,128)(2,1)} fusion(bf16[1024,512]{0,1:T(8,128)(2,1)} %all-gather.3.cloned.1.call-done, bf16[512,2048]{1,0:T(8,128)(2,1)} %all-gather.5.cloned.1.call-done), kind=kOutput, calls=%fused_computation | convolution fusion | flops 2149580800 | bytes 7340032 | tf_op jit(solution)/shard_map/dot_general | solution.py:10
Async XLA Ops:
  6.5 69.8 %all-gather.3.cloned.1.call-start = ((), (), s32[]{:S(2)}) async-start(), calls=%async_computation | async-start | bytes 1114112 | tf_op jit(solution)/shard_map/all_gather | solution.py:8
  7.3 138.2 %all-gather.5.cloned.1.call-start = ((), (), s32[]{:S(2)}) async-start(), calls=%async_computation.1 | async-start | bytes 2162688 | tf_op jit(solution)/shard_map/all_gather | solution.py:9
Sparse Core Ops, SparseCore 0:
  9.4 66.8 all-gather.2
  79.5 65.8 all-gather.4
where the time goes:
time: 159 us
  waiting for transfers between devices  139 us (87%)
  between operations  13.4 us (8%)
  matrix products  6.32 us (4%)
    all_gather x1, waiting for transfers between devices, on_device(): all_rows = lax.all_gather(rotation, 'grid', axis=0, tiled=True)  69.1 us
    all_gather x1, waiting for transfers between devices, on_device(): all_cols = lax.all_gather(orbitals, 'band', axis=1, tiled=True)  68.3 us
    dot_general x1, matrix products, on_device(): total = jnp.dot(all_cols, all_rows, preferred_element_type=jnp.float32)  6.32 us
  transfers between devices with their start and end apart: 2, of which 2 were waited for; matrix products, arithmetic and copies ran while one was open for 0% of the time, Pallas kernels for 0%

commit v1 on v0

--- a/solution.py
+++ b/solution.py
@@ -4,8 +4,19 @@
 from jax.sharding import PartitionSpec as P
 
 
+def around_the_ring(x, mesh_axis, dim):
+    size = lax.axis_size(mesh_axis)
+    right = [(i, (i + 1) % size) for i in range(size)]
+    blocks = [x]
+    for far in range(1, size):
+        blocks = [lax.ppermute(blocks[0], mesh_axis, right), *blocks]
+    whole = jnp.concatenate(blocks, axis=dim)
+    shift = (lax.axis_index(mesh_axis) + 1) * blocks[-1].shape[dim]
+    return jnp.roll(whole, shift, axis=dim)
+
+
 def on_device(orbitals, rotation):
-    all_cols = lax.all_gather(orbitals, "band", axis=1, tiled=True)
+    all_cols = around_the_ring(orbitals, "band", 1)
     all_rows = lax.all_gather(rotation, "grid", axis=0, tiled=True)
     total = jnp.dot(all_cols, all_rows, preferred_element_type=jnp.float32)
     return total.astype(jnp.bfloat16)

time: 159 us -> 147 us (0.925)
  waiting for transfers between devices: 139 us -> 95.2 us
  starting transfers between devices: 0.04 us -> 31.2 us
    ppermute x0 -> x15, waiting for transfers between devices: none -> 71.5 us  [around_the_ring(): blocks = [lax.ppermute(blocks[0], mesh_axis, right), *blocks]]
    all_gather x1 -> x0, waiting for transfers between devices: 68.3 us -> none  [on_device(): all_cols = lax.all_gather(orbitals, 'band', axis=1, tiled=True)]
    all_gather x1, waiting for transfers between devices: 69.1 us -> 23.7 us  [on_device(): all_rows = lax.all_gather(rotation, 'grid', axis=0, tiled=True)]
    ppermute x0 -> x15, starting transfers between devices: none -> 31.2 us  [around_the_ring(): blocks = [lax.ppermute(blocks[0], mesh_axis, right), *blocks]]
  transfers between devices with their start and end apart: 2 -> 16, of which waited for: 2 -> 16; matrix products, arithmetic and copies ran while one was open for 0% -> 0% of each run, Pallas kernels for 0% -> 0%
where the time goes in v1:
time: 147 us; the launch traced here: 146 us
  waiting for transfers between devices  95.2 us (65%)
  starting transfers between devices  31.2 us (21%)
  between operations  13.8 us (9%)
  matrix products  5.99 us (4%)
    ppermute x15, waiting for transfers between devices, around_the_ring(): blocks = [lax.ppermute(blocks[0], mesh_axis, right), *blocks]  71.5 us
    ppermute x15, starting transfers between devices, around_the_ring(): blocks = [lax.ppermute(blocks[0], mesh_axis, right), *blocks]  31.2 us
    all_gather x1, waiting for transfers between devices, on_device(): all_rows = lax.all_gather(rotation, 'grid', axis=0, tiled=True)  23.7 us
    dot_general x1, matrix products, on_device(): total = jnp.dot(all_cols, all_rows, preferred_element_type=jnp.float32)  5.99 us
  transfers between devices with their start and end apart: 16, of which 16 were waited for; matrix products, arithmetic and copies ran while one was open for 0% of the time, Pallas kernels for 0%

profile of v1, /device:TPU:1, one launch (start us, length us, event | category | flops | bytes accessed | tf_op | source)
XLA Modules:
  0.0 146.4 jit_solution(11834522624852118642)
XLA Ops:
  6.5 4.5 %collective-permute-start = (bf16[1024,32]{0,1:T(8,128)(2,1)}, bf16[1024,32]{0,1:T(8,128)(2,1)S(1)}, u32[]{:S(2)}, u32[]{:S(2)}) collective-permute-start(bf16[1024,32]{0,1:T(8,128)(2,1)} %param.2), channel_id=1, source_target_pairs={{0,1},{1,2},{2,3},{3,4},{4,5},{5,6},{6,7},{7,8},{8,9},{9,10},{10,1... | collective-permute-start | bytes 196616 | tf_op jit(solution)/shard_map/ppermute | solution.py:12
  11.0 9.4 %collective-permute-done = bf16[1024,32]{0,1:T(8,128)(2,1)S(1)} collective-permute-done((bf16[1024,32]{0,1:T(8,128)(2,1)}, bf16[1024,32]{0,1:T(8,128)(2,1)S(1)}, u32[]{:S(2)}, u32[]{:S(2)}) %collective-permute-start) | collective-permute-done | bytes 65568 | tf_op jit(solution)/shard_map/ppermute | solution.py:12
  20.5 1.9 %collective-permute-start.1 = (bf16[1024,32]{0,1:T(8,128)(2,1)S(1)}, bf16[1024,32]{0,1:T(8,128)(2,1)S(1)}, u32[]{:S(2)}, u32[]{:S(2)}) collective-permute-start(bf16[1024,32]{0,1:T(8,128)(2,1)S(1)} %collective-permute-done), channel_id=1, source_target_pairs={{0,1},{1,2},{2,3},{3,4},{4,5},{5,6},{6,7},{7,8},{8,9},{9,10},{10,1... | collective-permute-start | bytes 196616 | tf_op jit(solution)/shard_map/ppermute | solution.py:12
  22.4 4.3 %collective-permute-done.1 = bf16[1024,32]{0,1:T(8,128)(2,1)S(1)} collective-permute-done((bf16[1024,32]{0,1:T(8,128)(2,1)S(1)}, bf16[1024,32]{0,1:T(8,128)(2,1)S(1)}, u32[]{:S(2)}, u32[]{:S(2)}) %collective-permute-start.1) | collective-permute-done | bytes 65568 | tf_op jit(solution)/shard_map/ppermute | solution.py:12
  26.7 1.9 %collective-permute-start.2 = (bf16[1024,32]{0,1:T(8,128)(2,1)S(1)}, bf16[1024,32]{0,1:T(8,128)(2,1)S(1)}, u32[]{:S(2)}, u32[]{:S(2)}) collective-permute-start(bf16[1024,32]{0,1:T(8,128)(2,1)S(1)} %collective-permute-done.1), channel_id=1, source_target_pairs={{0,1},{1,2},{2,3},{3,4},{4,5},{5,6},{6,7},{7,8},{8,9},{9,10},{10,1... | collective-permute-start | bytes 196616 | tf_op jit(solution)/shard_map/ppermute | solution.py:12
  28.6 4.3 %collective-permute-done.2 = bf16[1024,32]{0,1:T(8,128)(2,1)S(1)} collective-permute-done((bf16[1024,32]{0,1:T(8,128)(2,1)S(1)}, bf16[1024,32]{0,1:T(8,128)(2,1)S(1)}, u32[]{:S(2)}, u32[]{:S(2)}) %collective-permute-start.2) | collective-permute-done | bytes 65568 | tf_op jit(solution)/shard_map/ppermute | solution.py:12
  32.9 1.9 %collective-permute-start.3 = (bf16[1024,32]{0,1:T(8,128)(2,1)S(1)}, bf16[1024,32]{0,1:T(8,128)(2,1)S(1)}, u32[]{:S(2)}, u32[]{:S(2)}) collective-permute-start(bf16[1024,32]{0,1:T(8,128)(2,1)S(1)} %collective-permute-done.2), channel_id=1, source_target_pairs={{0,1},{1,2},{2,3},{3,4},{4,5},{5,6},{6,7},{7,8},{8,9},{9,10},{10,1... | collective-permute-start | bytes 196616 | tf_op jit(solution)/shard_map/ppermute | solution.py:12
  34.8 4.3 %collective-permute-done.3 = bf16[1024,32]{0,1:T(8,128)(2,1)S(1)} collective-permute-done((bf16[1024,32]{0,1:T(8,128)(2,1)S(1)}, bf16[1024,32]{0,1:T(8,128)(2,1)S(1)}, u32[]{:S(2)}, u32[]{:S(2)}) %collective-permute-start.3) | collective-permute-done | bytes 65568 | tf_op jit(solution)/shard_map/ppermute | solution.py:12
  39.1 1.9 %collective-permute-start.4 = (bf16[1024,32]{0,1:T(8,128)(2,1)S(1)}, bf16[1024,32]{0,1:T(8,128)(2,1)S(1)}, u32[]{:S(2)}, u32[]{:S(2)}) collective-permute-start(bf16[1024,32]{0,1:T(8,128)(2,1)S(1)} %collective-permute-done.3), channel_id=1, source_target_pairs={{0,1},{1,2},{2,3},{3,4},{4,5},{5,6},{6,7},{7,8},{8,9},{9,10},{10,1... | collective-permute-start | bytes 196616 | tf_op jit(solution)/shard_map/ppermute | solution.py:12
  41.0 4.3 %collective-permute-done.4 = bf16[1024,32]{0,1:T(8,128)(2,1)S(1)} collective-permute-done((bf16[1024,32]{0,1:T(8,128)(2,1)S(1)}, bf16[1024,32]{0,1:T(8,128)(2,1)S(1)}, u32[]{:S(2)}, u32[]{:S(2)}) %collective-permute-start.4) | collective-permute-done | bytes 65568 | tf_op jit(solution)/shard_map/ppermute | solution.py:12
  45.3 1.9 %collective-permute-start.5 = (bf16[1024,32]{0,1:T(8,128)(2,1)S(1)}, bf16[1024,32]{0,1:T(8,128)(2,1)S(1)}, u32[]{:S(2)}, u32[]{:S(2)}) collective-permute-start(bf16[1024,32]{0,1:T(8,128)(2,1)S(1)} %collective-permute-done.4), channel_id=1, source_target_pairs={{0,1},{1,2},{2,3},{3,4},{4,5},{5,6},{6,7},{7,8},{8,9},{9,10},{10,1... | collective-permute-start | bytes 196616 | tf_op jit(solution)/shard_map/ppermute | solution.py:12
  47.2 4.3 %collective-permute-done.5 = bf16[1024,32]{0,1:T(8,128)(2,1)S(1)} collective-permute-done((bf16[1024,32]{0,1:T(8,128)(2,1)S(1)}, bf16[1024,32]{0,1:T(8,128)(2,1)S(1)}, u32[]{:S(2)}, u32[]{:S(2)}) %collective-permute-start.5) | collective-permute-done | bytes 65568 | tf_op jit(solution)/shard_map/ppermute | solution.py:12
  51.5 1.9 %collective-permute-start.6 = (bf16[1024,32]{0,1:T(8,128)(2,1)S(1)}, bf16[1024,32]{0,1:T(8,128)(2,1)S(1)}, u32[]{:S(2)}, u32[]{:S(2)}) collective-permute-start(bf16[1024,32]{0,1:T(8,128)(2,1)S(1)} %collective-permute-done.5), channel_id=1, source_target_pairs={{0,1},{1,2},{2,3},{3,4},{4,5},{5,6},{6,7},{7,8},{8,9},{9,10},{10,1... | collective-permute-start | bytes 196616 | tf_op jit(solution)/shard_map/ppermute | solution.py:12
  53.4 5.0 %collective-permute-done.6 = bf16[1024,32]{0,1:T(8,128)(2,1)S(1)} collective-permute-done((bf16[1024,32]{0,1:T(8,128)(2,1)S(1)}, bf16[1024,32]{0,1:T(8,128)(2,1)S(1)}, u32[]{:S(2)}, u32[]{:S(2)}) %collective-permute-start.6) | collective-permute-done | bytes 65568 | tf_op jit(solution)/shard_map/ppermute | solution.py:12
  58.4 1.9 %collective-permute-start.7 = (bf16[1024,32]{0,1:T(8,128)(2,1)S(1)}, bf16[1024,32]{0,1:T(8,128)(2,1)S(1)}, u32[]{:S(2)}, u32[]{:S(2)}) collective-permute-start(bf16[1024,32]{0,1:T(8,128)(2,1)S(1)} %collective-permute-done.6), channel_id=1, source_target_pairs={{0,1},{1,2},{2,3},{3,4},{4,5},{5,6},{6,7},{7,8},{8,9},{9,10},{10,1... | collective-permute-start | bytes 196616 | tf_op jit(solution)/shard_map/ppermute | solution.py:12
  60.3 4.3 %collective-permute-done.7 = bf16[1024,32]{0,1:T(8,128)(2,1)S(1)} collective-permute-done((bf16[1024,32]{0,1:T(8,128)(2,1)S(1)}, bf16[1024,32]{0,1:T(8,128)(2,1)S(1)}, u32[]{:S(2)}, u32[]{:S(2)}) %collective-permute-start.7) | collective-permute-done | bytes 65568 | tf_op jit(solution)/shard_map/ppermute | solution.py:12
  64.6 1.9 %collective-permute-start.8 = (bf16[1024,32]{0,1:T(8,128)(2,1)S(1)}, bf16[1024,32]{0,1:T(8,128)(2,1)S(1)}, u32[]{:S(2)}, u32[]{:S(2)}) collective-permute-start(bf16[1024,32]{0,1:T(8,128)(2,1)S(1)} %collective-permute-done.7), channel_id=1, source_target_pairs={{0,1},{1,2},{2,3},{3,4},{4,5},{5,6},{6,7},{7,8},{8,9},{9,10},{10,1... | collective-permute-start | bytes 196616 | tf_op jit(solution)/shard_map/ppermute | solution.py:12
  66.6 4.3 %collective-permute-done.8 = bf16[1024,32]{0,1:T(8,128)(2,1)S(1)} collective-permute-done((bf16[1024,32]{0,1:T(8,128)(2,1)S(1)}, bf16[1024,32]{0,1:T(8,128)(2,1)S(1)}, u32[]{:S(2)}, u32[]{:S(2)}) %collective-permute-start.8) | collective-permute-done | bytes 65568 | tf_op jit(solution)/shard_map/ppermute | solution.py:12
  70.8 1.9 %collective-permute-start.9 = (bf16[1024,32]{0,1:T(8,128)(2,1)S(1)}, bf16[1024,32]{0,1:T(8,128)(2,1)S(1)}, u32[]{:S(2)}, u32[]{:S(2)}) collective-permute-start(bf16[1024,32]{0,1:T(8,128)(2,1)S(1)} %collective-permute-done.8), channel_id=1, source_target_pairs={{0,1},{1,2},{2,3},{3,4},{4,5},{5,6},{6,7},{7,8},{8,9},{9,10},{10,1... | collective-permute-start | bytes 196616 | tf_op jit(solution)/shard_map/ppermute | solution.py:12
  72.8 4.3 %collective-permute-done.9 = bf16[1024,32]{0,1:T(8,128)(2,1)S(1)} collective-permute-done((bf16[1024,32]{0,1:T(8,128)(2,1)S(1)}, bf16[1024,32]{0,1:T(8,128)(2,1)S(1)}, u32[]{:S(2)}, u32[]{:S(2)}) %collective-permute-start.9) | collective-permute-done | bytes 65568 | tf_op jit(solution)/shard_map/ppermute | solution.py:12
  77.0 1.9 %collective-permute-start.10 = (bf16[1024,32]{0,1:T(8,128)(2,1)S(1)}, bf16[1024,32]{0,1:T(8,128)(2,1)S(1)}, u32[]{:S(2)}, u32[]{:S(2)}) collective-permute-start(bf16[1024,32]{0,1:T(8,128)(2,1)S(1)} %collective-permute-done.9), channel_id=1, source_target_pairs={{0,1},{1,2},{2,3},{3,4},{4,5},{5,6},{6,7},{7,8},{8,9},{9,10},{10,1... | collective-permute-start | bytes 196616 | tf_op jit(solution)/shard_map/ppermute | solution.py:12
  79.0 4.3 %collective-permute-done.10 = bf16[1024,32]{0,1:T(8,128)(2,1)S(1)} collective-permute-done((bf16[1024,32]{0,1:T(8,128)(2,1)S(1)}, bf16[1024,32]{0,1:T(8,128)(2,1)S(1)}, u32[]{:S(2)}, u32[]{:S(2)}) %collective-permute-start.10) | collective-permute-done | bytes 65568 | tf_op jit(solution)/shard_map/ppermute | solution.py:12
  83.3 1.9 %collective-permute-start.11 = (bf16[1024,32]{0,1:T(8,128)(2,1)S(1)}, bf16[1024,32]{0,1:T(8,128)(2,1)S(1)}, u32[]{:S(2)}, u32[]{:S(2)}) collective-permute-start(bf16[1024,32]{0,1:T(8,128)(2,1)S(1)} %collective-permute-done.10), channel_id=1, source_target_pairs={{0,1},{1,2},{2,3},{3,4},{4,5},{5,6},{6,7},{7,8},{8,9},{9,10},{10,1... | collective-permute-start | bytes 196616 | tf_op jit(solution)/shard_map/ppermute | solution.py:12
  85.2 4.3 %collective-permute-done.11 = bf16[1024,32]{0,1:T(8,128)(2,1)S(1)} collective-permute-done((bf16[1024,32]{0,1:T(8,128)(2,1)S(1)}, bf16[1024,32]{0,1:T(8,128)(2,1)S(1)}, u32[]{:S(2)}, u32[]{:S(2)}) %collective-permute-start.11) | collective-permute-done | bytes 65568 | tf_op jit(solution)/shard_map/ppermute | solution.py:12
  89.5 1.9 %collective-permute-start.12 = (bf16[1024,32]{0,1:T(8,128)(2,1)S(1)}, bf16[1024,32]{0,1:T(8,128)(2,1)S(1)}, u32[]{:S(2)}, u32[]{:S(2)}) collective-permute-start(bf16[1024,32]{0,1:T(8,128)(2,1)S(1)} %collective-permute-done.11), channel_id=1, source_target_pairs={{0,1},{1,2},{2,3},{3,4},{4,5},{5,6},{6,7},{7,8},{8,9},{9,10},{10,1... | collective-permute-start | bytes 196616 | tf_op jit(solution)/shard_map/ppermute | solution.py:12
  91.4 4.9 %collective-permute-done.12 = bf16[1024,32]{0,1:T(8,128)(2,1)S(1)} collective-permute-done((bf16[1024,32]{0,1:T(8,128)(2,1)S(1)}, bf16[1024,32]{0,1:T(8,128)(2,1)S(1)}, u32[]{:S(2)}, u32[]{:S(2)}) %collective-permute-start.12) | collective-permute-done | bytes 65568 | tf_op jit(solution)/shard_map/ppermute | solution.py:12
  96.3 1.9 %collective-permute-start.13 = (bf16[1024,32]{0,1:T(8,128)(2,1)S(1)}, bf16[1024,32]{0,1:T(8,128)(2,1)S(1)}, u32[]{:S(2)}, u32[]{:S(2)}) collective-permute-start(bf16[1024,32]{0,1:T(8,128)(2,1)S(1)} %collective-permute-done.12), channel_id=1, source_target_pairs={{0,1},{1,2},{2,3},{3,4},{4,5},{5,6},{6,7},{7,8},{8,9},{9,10},{10,1... | collective-permute-start | bytes 196616 | tf_op jit(solution)/shard_map/ppermute | solution.py:12
  98.2 5.0 %collective-permute-done.13 = bf16[1024,32]{0,1:T(8,128)(2,1)S(1)} collective-permute-done((bf16[1024,32]{0,1:T(8,128)(2,1)S(1)}, bf16[1024,32]{0,1:T(8,128)(2,1)S(1)}, u32[]{:S(2)}, u32[]{:S(2)}) %collective-permute-start.13) | collective-permute-done | bytes 65568 | tf_op jit(solution)/shard_map/ppermute | solution.py:12
  103.2 1.9 %collective-permute-start.14 = (bf16[1024,32]{0,1:T(8,128)(2,1)S(1)}, bf16[1024,32]{0,1:T(8,128)(2,1)S(1)}, u32[]{:S(2)}, u32[]{:S(2)}) collective-permute-start(bf16[1024,32]{0,1:T(8,128)(2,1)S(1)} %collective-permute-done.13), channel_id=1, source_target_pairs={{0,1},{1,2},{2,3},{3,4},{4,5},{5,6},{6,7},{7,8},{8,9},{9,10},{10,1... | collective-permute-start | bytes 196616 | tf_op jit(solution)/shard_map/ppermute | solution.py:12
  105.2 4.3 %collective-permute-done.14 = bf16[1024,32]{0,1:T(8,128)(2,1)S(1)} collective-permute-done((bf16[1024,32]{0,1:T(8,128)(2,1)S(1)}, bf16[1024,32]{0,1:T(8,128)(2,1)S(1)}, u32[]{:S(2)}, u32[]{:S(2)}) %collective-permute-start.14) | collective-permute-done | bytes 65568 | tf_op jit(solution)/shard_map/ppermute | solution.py:12
  109.9 23.7 %all-gather.2.cloned.1.call-done = bf16[512,2048]{1,0:T(8,128)(2,1)} async-done(((bf16[16,2048]{1,0:T(8,128)(2,1)}), bf16[512,2048]{1,0:T(8,128)(2,1)}) %all-gather.2.cloned.1.call-update) | async-done | bytes 2097168 | tf_op jit(solution)/shard_map/all_gather | solution.py:20
  133.6 6.0 %convolution_convert_fusion = bf16[1024,2048]{1,0:T(8,128)(2,1)} fusion(bf16[512,2048]{1,0:T(8,128)(2,1)} %all-gather.2.cloned.1.call-done, bf16[1024,1024]{0,1:T(8,128)(2,1)S(1)} %constant_dynamic-update-slice_fusion, s32[]{:T(128)S(6)} %select_n.14), kind=kOutput, calls=%fused_computation | convolution fusion | flops 2149580800 | bytes 7340036 | tf_op jit(solution)/shard_map/dot_general | solution.py:21
  (36 shorter events, 0.2 us)
Async XLA Ops:
  6.5 103.1 %copy-start = (bf16[1024,32]{0,1:T(8,128)(2,1)S(1)}, bf16[1024,32]{0,1:T(8,128)(2,1)}, u32[]{:S(2)}) copy-start(bf16[1024,32]{0,1:T(8,128)(2,1)} %param.2) | copy-start | bytes 196612
  6.5 127.0 %all-gather.2.cloned.1.call-start = ((), (), s32[]{:S(2)}) async-start(), calls=%async_computation | async-start | bytes 2162688 | tf_op jit(solution)/shard_map/all_gather | solution.py:20
  6.5 13.9 %collective-permute-start = (bf16[1024,32]{0,1:T(8,128)(2,1)}, bf16[1024,32]{0,1:T(8,128)(2,1)S(1)}, u32[]{:S(2)}, u32[]{:S(2)}) collective-permute-start(bf16[1024,32]{0,1:T(8,128)(2,1)} %param.2), channel_id=1, source_target_pairs={{0,1},{1,2},{2,3},{3,4},{4,5},{5,6},{6,7},{7,8},{8,9},{9,10},{10,1... | collective-permute-start | bytes 196616 | tf_op jit(solution)/shard_map/ppermute | solution.py:12
  20.5 6.2 %collective-permute-start.1 = (bf16[1024,32]{0,1:T(8,128)(2,1)S(1)}, bf16[1024,32]{0,1:T(8,128)(2,1)S(1)}, u32[]{:S(2)}, u32[]{:S(2)}) collective-permute-start(bf16[1024,32]{0,1:T(8,128)(2,1)S(1)} %collective-permute-done), channel_id=1, source_target_pairs={{0,1},{1,2},{2,3},{3,4},{4,5},{5,6},{6,7},{7,8},{8,9},{9,10},{10,1... | collective-permute-start | bytes 196616 | tf_op jit(solution)/shard_map/ppermute | solution.py:12
  26.7 6.2 %collective-permute-start.2 = (bf16[1024,32]{0,1:T(8,128)(2,1)S(1)}, bf16[1024,32]{0,1:T(8,128)(2,1)S(1)}, u32[]{:S(2)}, u32[]{:S(2)}) collective-permute-start(bf16[1024,32]{0,1:T(8,128)(2,1)S(1)} %collective-permute-done.1), channel_id=1, source_target_pairs={{0,1},{1,2},{2,3},{3,4},{4,5},{5,6},{6,7},{7,8},{8,9},{9,10},{10,1... | collective-permute-start | bytes 196616 | tf_op jit(solution)/shard_map/ppermute | solution.py:12
  32.9 6.2 %collective-permute-start.3 = (bf16[1024,32]{0,1:T(8,128)(2,1)S(1)}, bf16[1024,32]{0,1:T(8,128)(2,1)S(1)}, u32[]{:S(2)}, u32[]{:S(2)}) collective-permute-start(bf16[1024,32]{0,1:T(8,128)(2,1)S(1)} %collective-permute-done.2), channel_id=1, source_target_pairs={{0,1},{1,2},{2,3},{3,4},{4,5},{5,6},{6,7},{7,8},{8,9},{9,10},{10,1... | collective-permute-start | bytes 196616 | tf_op jit(solution)/shard_map/ppermute | solution.py:12
  39.1 6.2 %collective-permute-start.4 = (bf16[1024,32]{0,1:T(8,128)(2,1)S(1)}, bf16[1024,32]{0,1:T(8,128)(2,1)S(1)}, u32[]{:S(2)}, u32[]{:S(2)}) collective-permute-start(bf16[1024,32]{0,1:T(8,128)(2,1)S(1)} %collective-permute-done.3), channel_id=1, source_target_pairs={{0,1},{1,2},{2,3},{3,4},{4,5},{5,6},{6,7},{7,8},{8,9},{9,10},{10,1... | collective-permute-start | bytes 196616 | tf_op jit(solution)/shard_map/ppermute | solution.py:12
  45.3 6.2 %collective-permute-start.5 = (bf16[1024,32]{0,1:T(8,128)(2,1)S(1)}, bf16[1024,32]{0,1:T(8,128)(2,1)S(1)}, u32[]{:S(2)}, u32[]{:S(2)}) collective-permute-start(bf16[1024,32]{0,1:T(8,128)(2,1)S(1)} %collective-permute-done.4), channel_id=1, source_target_pairs={{0,1},{1,2},{2,3},{3,4},{4,5},{5,6},{6,7},{7,8},{8,9},{9,10},{10,1... | collective-permute-start | bytes 196616 | tf_op jit(solution)/shard_map/ppermute | solution.py:12
  51.5 6.9 %collective-permute-start.6 = (bf16[1024,32]{0,1:T(8,128)(2,1)S(1)}, bf16[1024,32]{0,1:T(8,128)(2,1)S(1)}, u32[]{:S(2)}, u32[]{:S(2)}) collective-permute-start(bf16[1024,32]{0,1:T(8,128)(2,1)S(1)} %collective-permute-done.5), channel_id=1, source_target_pairs={{0,1},{1,2},{2,3},{3,4},{4,5},{5,6},{6,7},{7,8},{8,9},{9,10},{10,1... | collective-permute-start | bytes 196616 | tf_op jit(solution)/shard_map/ppermute | solution.py:12
  58.4 6.2 %collective-permute-start.7 = (bf16[1024,32]{0,1:T(8,128)(2,1)S(1)}, bf16[1024,32]{0,1:T(8,128)(2,1)S(1)}, u32[]{:S(2)}, u32[]{:S(2)}) collective-permute-start(bf16[1024,32]{0,1:T(8,128)(2,1)S(1)} %collective-permute-done.6), channel_id=1, source_target_pairs={{0,1},{1,2},{2,3},{3,4},{4,5},{5,6},{6,7},{7,8},{8,9},{9,10},{10,1... | collective-permute-start | bytes 196616 | tf_op jit(solution)/shard_map/ppermute | solution.py:12
  64.6 6.2 %collective-permute-start.8 = (bf16[1024,32]{0,1:T(8,128)(2,1)S(1)}, bf16[1024,32]{0,1:T(8,128)(2,1)S(1)}, u32[]{:S(2)}, u32[]{:S(2)}) collective-permute-start(bf16[1024,32]{0,1:T(8,128)(2,1)S(1)} %collective-permute-done.7), channel_id=1, source_target_pairs={{0,1},{1,2},{2,3},{3,4},{4,5},{5,6},{6,7},{7,8},{8,9},{9,10},{10,1... | collective-permute-start | bytes 196616 | tf_op jit(solution)/shard_map/ppermute | solution.py:12
  70.8 6.2 %collective-permute-start.9 = (bf16[1024,32]{0,1:T(8,128)(2,1)S(1)}, bf16[1024,32]{0,1:T(8,128)(2,1)S(1)}, u32[]{:S(2)}, u32[]{:S(2)}) collective-permute-start(bf16[1024,32]{0,1:T(8,128)(2,1)S(1)} %collective-permute-done.8), channel_id=1, source_target_pairs={{0,1},{1,2},{2,3},{3,4},{4,5},{5,6},{6,7},{7,8},{8,9},{9,10},{10,1... | collective-permute-start | bytes 196616 | tf_op jit(solution)/shard_map/ppermute | solution.py:12
  77.0 6.2 %collective-permute-start.10 = (bf16[1024,32]{0,1:T(8,128)(2,1)S(1)}, bf16[1024,32]{0,1:T(8,128)(2,1)S(1)}, u32[]{:S(2)}, u32[]{:S(2)}) collective-permute-start(bf16[1024,32]{0,1:T(8,128)(2,1)S(1)} %collective-permute-done.9), channel_id=1, source_target_pairs={{0,1},{1,2},{2,3},{3,4},{4,5},{5,6},{6,7},{7,8},{8,9},{9,10},{10,1... | collective-permute-start | bytes 196616 | tf_op jit(solution)/shard_map/ppermute | solution.py:12
  83.3 6.2 %collective-permute-start.11 = (bf16[1024,32]{0,1:T(8,128)(2,1)S(1)}, bf16[1024,32]{0,1:T(8,128)(2,1)S(1)}, u32[]{:S(2)}, u32[]{:S(2)}) collective-permute-start(bf16[1024,32]{0,1:T(8,128)(2,1)S(1)} %collective-permute-done.10), channel_id=1, source_target_pairs={{0,1},{1,2},{2,3},{3,4},{4,5},{5,6},{6,7},{7,8},{8,9},{9,10},{10,1... | collective-permute-start | bytes 196616 | tf_op jit(solution)/shard_map/ppermute | solution.py:12
  89.5 6.9 %collective-permute-start.12 = (bf16[1024,32]{0,1:T(8,128)(2,1)S(1)}, bf16[1024,32]{0,1:T(8,128)(2,1)S(1)}, u32[]{:S(2)}, u32[]{:S(2)}) collective-permute-start(bf16[1024,32]{0,1:T(8,128)(2,1)S(1)} %collective-permute-done.11), channel_id=1, source_target_pairs={{0,1},{1,2},{2,3},{3,4},{4,5},{5,6},{6,7},{7,8},{8,9},{9,10},{10,1... | collective-permute-start | bytes 196616 | tf_op jit(solution)/shard_map/ppermute | solution.py:12
  96.3 6.9 %collective-permute-start.13 = (bf16[1024,32]{0,1:T(8,128)(2,1)S(1)}, bf16[1024,32]{0,1:T(8,128)(2,1)S(1)}, u32[]{:S(2)}, u32[]{:S(2)}) collective-permute-start(bf16[1024,32]{0,1:T(8,128)(2,1)S(1)} %collective-permute-done.12), channel_id=1, source_target_pairs={{0,1},{1,2},{2,3},{3,4},{4,5},{5,6},{6,7},{7,8},{8,9},{9,10},{10,1... | collective-permute-start | bytes 196616 | tf_op jit(solution)/shard_map/ppermute | solution.py:12
  103.2 6.2 %collective-permute-start.14 = (bf16[1024,32]{0,1:T(8,128)(2,1)S(1)}, bf16[1024,32]{0,1:T(8,128)(2,1)S(1)}, u32[]{:S(2)}, u32[]{:S(2)}) collective-permute-start(bf16[1024,32]{0,1:T(8,128)(2,1)S(1)} %collective-permute-done.13), channel_id=1, source_target_pairs={{0,1},{1,2},{2,3},{3,4},{4,5},{5,6},{6,7},{7,8},{8,9},{9,10},{10,1... | collective-permute-start | bytes 196616 | tf_op jit(solution)/shard_map/ppermute | solution.py:12
Sparse Core Ops, SparseCore 0:
  66.7 66.8 all-gather.1
